TPU v7x, 32 devices: a whole 2x2x4 slice. The times are simulated.
32 devices in a mesh: pair: 8 (over z, y), chan: 4 (over x, core).
Axes of the slice: x: 2, y: 2, z: 4, core: 2. Of those that a mesh axis runs over, the one named last changes fastest.
Arguments:
- jones_init: float32 [512, 4, 128], P('pair', 'chan'), may hold values from -2 to 2
- dual_init: float32 [512, 4, 128], P('pair', 'chan'), may hold values from -1.2 to 1.2
- penalty: float32 [16], replicated, may hold values from 0.5 to 5
- sky_flux: float32 [4, 4, 16], P('chan'), may hold values from -0.1 to 0.5, as said below
- visibility: bfloat16 [8, 4, 8, 2, 128, 128], P('pair', 'chan'), may hold values from -4 to 4
- phases: float32 [8, 8, 2, 1024], P('pair'), may hold values from -3.1416 to 3.1416, as said below
- pair_ids: int32 [8], P('pair'), may hold values from 0 to 35, as said below
- counts: int32 [8], P('pair'), may hold values from 2 to 8, as said below
- slot_flags: int32 [8, 8], P('pair'), may hold values 0 or 1
Outputs:
- jones_final: float32 [512, 4, 128], P('pair', 'chan')
- duals_final: float32 [512, 4, 128], P('pair', 'chan')
- consensus: float32 [512, 3, 128], P('pair')
Inputs may be any that keep to these rules, and one draw needn't show every extreme that they name: `sky_flux`: [f, 0, k] and [f, 1, k] are the two polarized fluxes, [f, 2, k] and [f, 3, k] the real and imaginary cross terms. `phases`: [t, s, 0, k * 64 + p] is the phase of direction k at row station p in slot s, [t, s, 1, ...] that at column station p, before scaling by frequency. `pair_ids`: block pair of each tile, numbered row by row over blocks a <= b of 8. A tile keeps slots 0 to counts - 1; tiles whose column block lies 8 // 2 or more blocks after their row block keep all 8.
All inputs are finite; a program needn't handle non-finite values. No bound on the sum of `slot_flags` on one device may be relied on, other than what follows from the above.
Results may differ from a plain program's by a relative error of at most 0.00076.
Values sent between devices are 32-bit elements; how exact they have to be, the bound alone decides.
A program may use at most 64 MiB of HBM per device.

v0:
```python
import jax
import jax.numpy as jnp
import numpy as np
from jax import lax
from jax.sharding import PartitionSpec as P

STATIONS = 512
DIRS = 16
BLOCK = 64
TIME = 8
NPOLY = 3
ITERS = 2
STEP_SCALE = 0.3
FULL_PRECISION = lax.Precision.HIGHEST


def pair_tables(block_count):
    row_list = []
    col_list = []
    for row_block in range(block_count):
        for col_block in range(row_block, block_count):
            row_list.append(row_block)
            col_list.append(col_block)
    return (np.array(row_list, np.int32), np.array(col_list, np.int32))


def split_parts(block_jones):
    station_count = block_jones.shape[0]
    chan_count = block_jones.shape[1]
    shaped = block_jones.reshape(station_count, chan_count, 2, 2, 2, DIRS)
    shaped = jnp.transpose(shaped, (2, 1, 0, 3, 5, 4))
    return (shaped[0], shaped[1])


def sky_parts(sky_flux):
    flux_xx = sky_flux[:, 0]
    flux_yy = sky_flux[:, 1]
    cross_re = sky_flux[:, 2]
    cross_im = sky_flux[:, 3]
    zeros_k = jnp.zeros_like(flux_xx)
    real_part = jnp.stack(
        [jnp.stack([flux_xx, cross_re], -1), jnp.stack([cross_re, flux_yy], -1)], -2
    )
    imag_part = jnp.stack(
        [jnp.stack([zeros_k, cross_im], -1), jnp.stack([-cross_im, zeros_k], -1)], -2
    )
    return (real_part, imag_part)


def times_sky(parts, sky_pair):
    jones_re = parts[0][..., None]
    jones_im = parts[1][..., None]
    sky_re = sky_pair[0][:, None, None]
    sky_im = sky_pair[1][:, None, None]
    out_re = jnp.sum(jones_re * sky_re - jones_im * sky_im, axis=-2)
    out_im = jnp.sum(jones_re * sky_im + jones_im * sky_re, axis=-2)
    return (out_re, out_im)


def phase_angles(theta_side, freq_ratio):
    slot_count = theta_side.shape[0]
    shaped = jnp.transpose(theta_side.reshape(slot_count, DIRS, BLOCK), (0, 2, 1))
    angle_all = freq_ratio[:, None, None, None] * shaped[None]
    angle_all = angle_all[:, :, :, None, :, None]
    return (jnp.cos(angle_all), jnp.sin(angle_all))


def rotate_flat(parts, cosines, sines):
    part_re = parts[0][:, None]
    part_im = parts[1][:, None]
    out_re = cosines * part_re - sines * part_im
    out_im = cosines * part_im + sines * part_re
    chan_count = out_re.shape[0]
    slot_count = out_re.shape[1]
    return (
        out_re.reshape(chan_count, slot_count, 2 * BLOCK, 2 * DIRS).astype(jnp.bfloat16),
        out_im.reshape(chan_count, slot_count, 2 * BLOCK, 2 * DIRS).astype(jnp.bfloat16),
    )


def unrotate(product, cosines, sines):
    chan_count = product.shape[0]
    slot_count = product.shape[1]
    shaped = product.reshape(chan_count, slot_count, BLOCK, 2, 2, DIRS, 2)
    neg_re = shaped[:, :, :, :, 0]
    neg_im = shaped[:, :, :, :, 1]
    grad_re = -jnp.sum(neg_re * cosines + neg_im * sines, axis=1)
    grad_im = -jnp.sum(neg_im * cosines - neg_re * sines, axis=1)
    both_parts = jnp.transpose(jnp.stack([grad_re, grad_im], 0), (2, 1, 0, 3, 5, 4))
    return both_parts.reshape(BLOCK, chan_count, 8 * DIRS)


def power_rows(parts):
    power = jnp.sum(parts[0] * parts[0] + parts[1] * parts[1], axis=2)
    power = jnp.transpose(power, (1, 0, 3, 2))
    return power.reshape(power.shape[0], -1)


def slot_terms(vis_part, weights, theta_part, freq_ratio, row_sky, col_sky, col_parts, mask_wide):
    cos_row, sin_row = phase_angles(theta_part[:, 0], freq_ratio)
    cos_col, sin_col = phase_angles(theta_part[:, 1], freq_ratio)
    left_re, left_im = rotate_flat(row_sky, cos_row, sin_row)
    right_re, right_im = rotate_flat(col_sky, cos_col, sin_col)
    conj_re, conj_im = rotate_flat(col_parts, cos_col, sin_col)
    left_side = jnp.concatenate([left_re, left_im], -1)
    model_rhs = jnp.stack(
        [jnp.concatenate([conj_re, conj_im], -1), jnp.concatenate([-conj_im, conj_re], -1)], 2
    )
    predicted = jnp.einsum(
        "ftpk,ftcqk->ftcpq", left_side, model_rhs, preferred_element_type=jnp.float32
    )
    weighting = weights[None, :, None, None, None] * mask_wide
    residual = (weighting * (vis_part.astype(jnp.float32) - predicted)).astype(jnp.bfloat16)
    row_rhs = jnp.stack(
        [jnp.concatenate([right_re, right_im], -1), jnp.concatenate([-right_im, right_re], -1)], 2
    )
    col_rhs = jnp.stack(
        [jnp.concatenate([left_re, left_im], -1), jnp.concatenate([left_im, -left_re], -1)], 2
    )
    row_out = jnp.einsum("ftcpq,ftcqk->ftpk", residual, row_rhs, preferred_element_type=jnp.float32)
    col_out = jnp.einsum("ftcpq,ftcpk->ftqk", residual, col_rhs, preferred_element_type=jnp.float32)
    return (unrotate(row_out, cos_row, sin_row), unrotate(col_out, cos_col, sin_col))


def tile_terms(
    full_jones, sky_pair, freq_ratio, tables, vis_tile, theta_tile, pair_id, kept_slots, flag_row
):
    pair_range = jnp.arange(tables[0].shape[0])
    row_block = jnp.sum(jnp.where(pair_range == pair_id, tables[0], 0)).astype(jnp.int32)
    col_block = jnp.sum(jnp.where(pair_range == pair_id, tables[1], 0)).astype(jnp.int32)
    row_jones = lax.dynamic_slice_in_dim(full_jones, row_block * BLOCK, BLOCK, 0)
    col_jones = lax.dynamic_slice_in_dim(full_jones, col_block * BLOCK, BLOCK, 0)
    row_sky = times_sky(split_parts(row_jones), sky_pair)
    col_parts = split_parts(col_jones)
    col_sky = times_sky(col_parts, sky_pair)
    station_rank = jnp.arange(BLOCK)
    strict = (station_rank[:, None] < station_rank[None, :]) | (row_block != col_block)
    pair_mask = strict.astype(jnp.float32)
    mask_wide = jnp.broadcast_to(pair_mask[:, None, :, None], (BLOCK, 2, BLOCK, 2)).reshape(
        2 * BLOCK, 2 * BLOCK
    )
    weights = flag_row.astype(jnp.float32) * (jnp.arange(TIME) < kept_slots).astype(jnp.float32)
    samples = jnp.sum(weights)
    chan_count = full_jones.shape[1]
    row_grad, col_grad = slot_terms(
        vis_tile, weights, theta_tile, freq_ratio, row_sky, col_sky, col_parts, mask_wide
    )
    row_curv = samples * jnp.dot(pair_mask, power_rows(col_sky), precision=FULL_PRECISION)
    col_curv = samples * jnp.dot(pair_mask.T, power_rows(row_sky), precision=FULL_PRECISION)
    return (
        row_block,
        col_block,
        row_grad,
        col_grad,
        row_curv.reshape(BLOCK, chan_count, 2 * DIRS),
        col_curv.reshape(BLOCK, chan_count, 2 * DIRS),
    )


def add_block(total, start, piece):
    current = lax.dynamic_slice_in_dim(total, start, piece.shape[0], 0)
    return lax.dynamic_update_slice_in_dim(total, current + piece, start, 0)


def data_terms(
    full_jones, sky_pair, freq_ratio, tables, visibility, phases, pair_ids, counts, slot_flags
):
    station_count = full_jones.shape[0]
    chan_count = full_jones.shape[1]
    grad_zero = jnp.zeros((station_count, chan_count, 8 * DIRS), jnp.float32)
    curv_zero = jnp.zeros((station_count, chan_count, 2 * DIRS), jnp.float32)

    def add_tile(carry, tile_inputs):
        grad_sum, curv_sum = carry
        vis_tile, theta_tile, pair_id, kept_slots, flag_row = tile_inputs
        row_block, col_block, row_grad, col_grad, row_curv, col_curv = tile_terms(
            full_jones,
            sky_pair,
            freq_ratio,
            tables,
            vis_tile,
            theta_tile,
            pair_id,
            kept_slots,
            flag_row,
        )
        grad_sum = add_block(grad_sum, row_block * BLOCK, row_grad)
        grad_sum = add_block(grad_sum, col_block * BLOCK, col_grad)
        curv_sum = add_block(curv_sum, row_block * BLOCK, row_curv)
        curv_sum = add_block(curv_sum, col_block * BLOCK, col_curv)
        return ((grad_sum, curv_sum), None)

    totals, unused = lax.scan(
        add_tile, (grad_zero, curv_zero), (visibility, phases, pair_ids, counts, slot_flags)
    )
    return totals


def cosine_basis(chan_total):
    middle = jnp.arange(chan_total, dtype=jnp.float32) + 0.5
    degree = jnp.arange(NPOLY, dtype=jnp.float32)
    normalizer = jnp.sqrt(jnp.where(degree == 0, 1.0, 2.0) / chan_total)
    return jnp.cos(jnp.pi * middle[:, None] * degree[None, :] / chan_total) * normalizer[None, :]


def project(values_all, poly_basis):
    return jnp.sum(poly_basis[None, :, :, None] * values_all[:, :, None, :], axis=1)


def expand(coefficients, poly_basis):
    return jnp.sum(poly_basis[None, :, :, None] * coefficients[:, None, :, :], axis=2)


def jacobi(jones_now, duals_now, gradient, curvature, penalty_full, target):
    divisor = jnp.tile(curvature, (1, 1, 4)) + 0.5 * penalty_full
    return (
        jones_now
        - STEP_SCALE
        * (gradient + 0.5 * penalty_full * (jones_now - target) + 0.5 * duals_now)
        / divisor
    )


def per_device(
    jones_init, dual_init, penalty, sky_flux, visibility, phases, pair_ids, counts, slot_flags
):
    chan_dev = jones_init.shape[1]
    chan_total = chan_dev * lax.axis_size("chan")
    chan_start = lax.axis_index("chan") * chan_dev
    freq_ratio = 1.0 + (chan_start + jnp.arange(chan_dev)).astype(jnp.float32) / chan_total
    poly_basis = lax.dynamic_slice_in_dim(cosine_basis(chan_total), chan_start, chan_dev, 0)
    penalty_full = jnp.tile(penalty, 8)
    sky_pair = sky_parts(sky_flux)
    row_table, col_table = pair_tables(STATIONS // BLOCK)
    tables = (jnp.asarray(row_table), jnp.asarray(col_table))

    def every_consensus(current, dual_now):
        return lax.psum(project(current + dual_now / penalty_full, poly_basis), "chan")

    jones_now, duals_now = (
        lax.all_gather(jones_init, "pair", axis=0, tiled=True),
        lax.all_gather(dual_init, "pair", axis=0, tiled=True),
    )
    center = every_consensus(jones_now, duals_now)
    for outer_round in range(ITERS):
        target = expand(center, poly_basis)
        grad_full, curv_full = data_terms(
            jones_now,
            sky_pair,
            freq_ratio,
            tables,
            visibility,
            phases,
            pair_ids,
            counts,
            slot_flags,
        )
        gradient, curvature = lax.psum((grad_full, curv_full), "pair")
        jones_now = jacobi(jones_now, duals_now, gradient, curvature, penalty_full, target)
        center = every_consensus(jones_now, duals_now)
        duals_now = duals_now + penalty_full * (jones_now - expand(center, poly_basis))
    own_rows = jones_init.shape[0]
    own_start = lax.axis_index("pair") * own_rows
    return (
        lax.dynamic_slice_in_dim(jones_now, own_start, own_rows, 0),
        lax.dynamic_slice_in_dim(duals_now, own_start, own_rows, 0),
        lax.dynamic_slice_in_dim(center, own_start, own_rows, 0),
    )


def solution(mesh):
    in_specs = (
        P("pair", "chan", None),
        P("pair", "chan", None),
        P(),
        P("chan", None, None),
        P("pair", "chan", None, None, None, None),
        P("pair", None, None, None),
        P("pair"),
        P("pair"),
        P("pair", None),
    )
    out_specs = (P("pair", "chan", None), P("pair", "chan", None), P("pair", None, None))
    return jax.shard_map(
        per_device, mesh=mesh, in_specs=in_specs, out_specs=out_specs, check_vma=False
    )
```

profile of v0, /device:TPU:0, one launch (start us, length us, event | category | flops | bytes accessed | tf_op | source)
XLA Modules:
  0.0 485.5 jit_solution(17189194167199863357)
XLA Ops:
  11.9 32.8 %all_gather.6 = f32[512,1,128]{2,1,0:T(1,128)S(1)} all-gather(f32[64,1,128]{2,1,0:T(1,128)} %param.11), channel_id=1, replica_groups=mesh['pair'=8,'chan'=4] {'pair'}, dimensions={0}, use_global_device_ids=true | all-gather | bytes 294912 | tf_op jit(solution)/shard_map/all_gather | solution.py:241
  47.9 2.9 cosine_reduce_fusion
  61.6 2.4 mul.1652
  64.0 2.7 copy.299
  67.1 2.4 mul.1658
  69.6 2.7 copy.302
  75.6 2.5 broadcast_in_dim.77
  78.1 4.2 mul.1646
  88.8 4.4 copy.330
  93.2 7.2 %add_reduce_fusion.2 = (f32[64,2,16,2]{3,2,1,0:T(8,128)S(1)}, f32[64,2,16,2]{3,2,1,0:T(8,128)}) fusion(f32[1,8,64,2,2,16,2]{1,6,5,4,3,2,0:T(2,128)} %bitcast.414, f32[8,64,16]{0,2,1:T(8,128)S(1)} %bitcast.426, f32[8,64,16]{0,2,1:T(8,128)S(1)} %bitcast.423), kind=kLoop, calls=%fused_computation.13 | loop fusion | flops 253952 | bytes 360448 | tf_op jit(solution)/shard_map/while/body/eval_jaxpr/reduce_sum | solution.py:87
  101.4 2.4 copy.332
  103.8 2.3 negate_bitcast_fusion.4
  106.2 2.4 copy.333
  111.3 4.4 copy.323
  115.7 7.4 %add_reduce_fusion.3 = (f32[64,2,16,2]{3,2,1,0:T(8,128)S(1)}, f32[64,2,16,2]{3,2,1,0:T(8,128)}) fusion(f32[1,8,64,2,2,16,2]{1,6,5,4,3,2,0:T(2,128)} %bitcast.415, f32[8,64,16]{0,2,1:T(8,128)S(1)} %bitcast.420, f32[8,64,16]{0,2,1:T(8,128)S(1)} %bitcast.417), kind=kLoop, calls=%fused_computation.15 | loop fusion | flops 253952 | bytes 360448 | tf_op jit(solution)/shard_map/while/body/eval_jaxpr/reduce_sum | solution.py:87
  124.2 1.8 copy.325
  126.0 2.3 negate_bitcast_fusion.6
  128.3 1.8 copy.326
  135.8 2.1 fusion.13
  140.2 31.0 %all_gather.7 = f32[512,1,128]{2,1,0:T(1,128)S(1)} all-gather(f32[64,1,128]{2,1,0:T(1,128)} %param.12), channel_id=1, replica_groups=mesh['pair'=8,'chan'=4] {'pair'}, dimensions={0}, use_global_device_ids=true | all-gather | bytes 294912 | tf_op jit(solution)/shard_map/all_gather | solution.py:242
  174.0 38.4 %all-reduce.18.cloned.1.call-done = (f32[512,1,128]{2,0,1:T(8,128)}, f32[512,32]{0,1:T(8,128)}) async-done(((f32[512,1,128]{2,0,1:T(8,128)}, f32[512,32]{0,1:T(8,128)}), (f32[512,1,128]{2,0,1:T(8,128)}, f32[512,32]{0,1:T(8,128)})) %all-reduce.18.cloned.1.call-update) | async-done | bytes 327696 | tf_op jit(solution)/shard_map/psum | solution.py:258
  212.4 1.6 tile.34
  214.0 1.8 copy.343
  215.8 33.2 %all-reduce.10.cloned.1.call-done = f32[512,3,128]{2,0,1:T(8,128)} async-done(((f32[512,3,128]{2,0,1:T(8,128)}), f32[512,3,128]{2,0,1:T(8,128)}) %all-reduce.10.cloned.1.call-update) | async-done | bytes 786448 | tf_op jit(solution)/shard_map/psum | solution.py:238
  250.3 1.9 add_bitcast_fusion.1
  260.3 2.1 copy.354
  262.5 1.7 mul.1758
  264.2 2.1 copy.356
  266.3 2.3 mul.1763
  268.6 1.7 fusion.58
  270.3 1.6 add_convert_fusion.1
  271.9 2.1 copy.360
  274.0 1.7 mul.1775
  275.7 2.1 copy.362
  277.9 2.3 mul.1780
  280.1 2.1 copy.346
  282.3 2.3 mul.1744
  284.6 2.1 copy.348
  286.7 2.3 mul.1747
  289.0 1.6 subtract_convert_fusion
  290.6 1.6 fusion.59
  296.9 4.6 copy.376
  301.6 6.2 %add_reduce_fusion = (f32[64,2,16,2]{3,2,1,0:T(8,128)S(1)}, f32[64,2,16,2]{3,2,1,0:T(8,128)S(1)}) fusion(f32[1,8,64,2,2,16,2]{1,6,5,4,3,2,0:T(2,128)} %bitcast.412, f32[8,64,16]{0,2,1:T(8,128)S(1)} %bitcast.427, f32[8,64,16]{0,2,1:T(8,128)S(1)} %bitcast.424), kind=kLoop, calls=%fused_computation.9 | loop fusion | flops 253952 | bytes 360448 | tf_op jit(solution)/shard_map/while/body/eval_jaxpr/reduce_sum | solution.py:87
  312.8 4.4 copy.368
  317.2 6.2 %add_reduce_fusion.1 = (f32[64,2,16,2]{3,2,1,0:T(8,128)S(1)}, f32[64,2,16,2]{3,2,1,0:T(8,128)S(1)}) fusion(f32[1,8,64,2,2,16,2]{1,6,5,4,3,2,0:T(2,128)} %bitcast.413, f32[8,64,16]{0,2,1:T(8,128)S(1)} %bitcast.421, f32[8,64,16]{0,2,1:T(8,128)S(1)} %bitcast.418), kind=kLoop, calls=%fused_computation.11 | loop fusion | flops 253952 | bytes 360448 | tf_op jit(solution)/shard_map/while/body/eval_jaxpr/reduce_sum | solution.py:87
  329.3 70.8 %all-reduce.16.cloned.1.call-done = (f32[512,32]{0,1:T(8,128)}, f32[512,1,128]{2,0,1:T(8,128)}) async-done(((f32[512,32]{0,1:T(8,128)}, f32[512,1,128]{2,0,1:T(8,128)}), (f32[512,32]{0,1:T(8,128)}, f32[512,1,128]{2,0,1:T(8,128)})) %all-reduce.16.cloned.1.call-update) | async-done | bytes 327696 | tf_op jit(solution)/shard_map/psum | solution.py:258
  401.0 35.5 %all-reduce.12.cloned.1.call-done = f32[512,3,128]{2,0,1:T(8,128)} async-done(((f32[512,3,128]{2,0,1:T(8,128)}), f32[512,3,128]{2,0,1:T(8,128)}) %all-reduce.12.cloned.1.call-update) | async-done | bytes 786448 | tf_op jit(solution)/shard_map/psum | solution.py:238
  440.0 35.2 %all-reduce.14.cloned.1.call-done = f32[512,3,128]{2,0,1:T(8,128)} async-done(((f32[512,3,128]{2,0,1:T(8,128)}), f32[512,3,128]{2,0,1:T(8,128)}) %all-reduce.14.cloned.1.call-update) | async-done | bytes 786448 | tf_op jit(solution)/shard_map/psum | solution.py:238
  (230 shorter events, 73.0 us)
Async XLA Ops:
  7.2 205.3 %all-reduce.18.cloned.1.call-start = ((), (), s32[]{:S(2)}) async-start(), calls=%async_computation.4 | async-start | bytes 655360 | tf_op jit(solution)/shard_map/psum | solution.py:258
  44.6 1.0 copy-start.3
  46.1 1.8 copy-start.17
  46.1 1.8 copy-start.19
  46.1 11.5 %copy-start.21 = (f32[64,2,16,2]{0,2,3,1:T(8,128)}, f32[64,2,16,2]{0,2,3,1:T(8,128)S(1)}, u32[]{:S(2)}) copy-start(f32[64,2,16,2]{0,2,3,1:T(8,128)S(1)} %get-tuple-element.97) | copy-start | bytes 49156
  46.1 12.4 %copy-start.23 = (f32[64,2,16,2]{0,2,3,1:T(8,128)}, f32[64,2,16,2]{0,2,3,1:T(8,128)S(1)}, u32[]{:S(2)}) copy-start(f32[64,2,16,2]{0,2,3,1:T(8,128)S(1)} %get-tuple-element.112) | copy-start | bytes 49156
  46.1 1.8 copy-start.34
  53.6 3.5 copy-start.1
  56.3 3.1 copy-start.2
  57.7 1.8 copy-start.31
  59.5 1.8 copy-start.33
  61.6 5.1 %copy-start.32 = (f32[8,1024]{1,0:T(8,128)S(1)}, f32[8,1024]{1,0:T(8,128)}, u32[]{:S(2)}) copy-start(f32[8,1024]{1,0:T(8,128)} %get-tuple-element.117) | copy-start | bytes 98308
  69.6 5.3 %copy-start.22 = (f32[64,2,16,2]{0,2,3,1:T(8,128)S(1)}, f32[64,2,16,2]{0,2,3,1:T(8,128)}, u32[]{:S(2)}) copy-start(f32[64,2,16,2]{0,2,3,1:T(8,128)} %copy-done.21) | copy-start | bytes 49156
  69.6 5.4 %copy-start.24 = (f32[64,2,16,2]{0,2,3,1:T(8,128)S(1)}, f32[64,2,16,2]{0,2,3,1:T(8,128)}, u32[]{:S(2)}) copy-start(f32[64,2,16,2]{0,2,3,1:T(8,128)} %copy-done.23) | copy-start | bytes 49156
  69.6 6.0 %copy-start.18 = (f32[64,2,16,2]{0,2,3,1:T(8,128)S(1)}, f32[64,2,16,2]{0,2,3,1:T(8,128)}, u32[]{:S(2)}) copy-start(f32[64,2,16,2]{0,2,3,1:T(8,128)} %copy-done.17) | copy-start | bytes 49156
  69.6 6.0 %copy-start.20 = (f32[64,2,16,2]{0,2,3,1:T(8,128)S(1)}, f32[64,2,16,2]{0,2,3,1:T(8,128)}, u32[]{:S(2)}) copy-start(f32[64,2,16,2]{0,2,3,1:T(8,128)} %copy-done.19) | copy-start | bytes 49156
  72.3 5.8 %copy-start = (f32[1,8,128,32]{2,3,1,0:T(8,128)}, f32[1,8,128,32]{2,3,1,0:T(8,128)S(1)}, u32[]{:S(2)}) copy-start(f32[1,8,128,32]{2,3,1,0:T(8,128)S(1)} %copy.302) | copy-start | bytes 393220
  78.1 5.6 %copy-start.15 = (bf16[1,1,8,2,128,128]{5,4,3,2,1,0:T(8,128)(2,1)S(1)}, bf16[1,1,8,2,128,128]{5,4,3,2,1,0:T(8,128)(2,1)}, u32[]{:S(2)}) copy-start(bf16[1,1,8,2,128,128]{5,4,3,2,1,0:T(8,128)(2,1)} %param.15) | copy-start | bytes 1572868
  78.1 8.2 %copy-start.11 = (bf16[1,8,128,32]{2,3,1,0:T(8,128)(2,1)S(1)}, bf16[1,8,128,32]{2,3,1,0:T(8,128)(2,1)}, u32[]{:S(2)}) copy-start(bf16[1,8,128,32]{2,3,1,0:T(8,128)(2,1)} %get-tuple-element.141) | copy-start | bytes 196612
  78.1 8.2 %copy-start.12 = (bf16[1,8,128,32]{2,3,1,0:T(8,128)(2,1)S(1)}, bf16[1,8,128,32]{2,3,1,0:T(8,128)(2,1)}, u32[]{:S(2)}) copy-start(bf16[1,8,128,32]{2,3,1,0:T(8,128)(2,1)} %add_convert_fusion.4) | copy-start | bytes 196612
  78.1 8.2 %copy-start.30 = (bf16[1,8,128,32]{2,3,1,0:T(8,128)(2,1)S(1)}, bf16[1,8,128,32]{2,3,1,0:T(8,128)(2,1)}, u32[]{:S(2)}) copy-start(bf16[1,8,128,32]{2,3,1,0:T(8,128)(2,1)} %get-tuple-element.140) | copy-start | bytes 196612
  87.7 0.8 copy-start.5
  101.4 8.6 %copy-start.25 = (bf16[1,8,128,32]{2,3,1,0:T(8,128)(2,1)S(1)}, bf16[1,8,128,32]{2,3,1,0:T(8,128)(2,1)}, u32[]{:S(2)}) copy-start(bf16[1,8,128,32]{2,3,1,0:T(8,128)(2,1)} %get-tuple-element.142) | copy-start | bytes 196612
  101.4 8.6 %copy-start.26 = (bf16[1,8,128,32]{2,3,1,0:T(8,128)(2,1)S(1)}, bf16[1,8,128,32]{2,3,1,0:T(8,128)(2,1)}, u32[]{:S(2)}) copy-start(bf16[1,8,128,32]{2,3,1,0:T(8,128)(2,1)} %get-tuple-element.143) | copy-start | bytes 196612
  101.4 8.6 %copy-start.27 = (bf16[1,8,128,32]{2,3,1,0:T(8,128)(2,1)S(1)}, bf16[1,8,128,32]{2,3,1,0:T(8,128)(2,1)}, u32[]{:S(2)}) copy-start(bf16[1,8,128,32]{2,3,1,0:T(8,128)(2,1)} %get-tuple-element.156) | copy-start | bytes 196612
  124.2 6.6 %copy-start.35 = (f32[64,16,2]{0,1,2:T(8,128)S(1)}, f32[64,16,2]{0,1,2:T(8,128)}, u32[]{:S(2)}) copy-start(f32[64,16,2]{0,1,2:T(8,128)} %add_reduce_fusion.11) | copy-start | bytes 24580
  132.4 7.0 %copy-start.8 = (f32[512,1,128]{2,0,1:T(8,128)}, f32[512,1,128]{2,0,1:T(8,128)S(1)}, u32[]{:S(2)}) copy-start(f32[512,1,128]{2,0,1:T(8,128)S(1)} %add_dynamic-update-slice_fusion.1) | copy-start | bytes 786436
  139.4 109.6 %all-reduce.10.cloned.1.call-start = ((), (), s32[]{:S(2)}) async-start(), calls=%async_computation | async-start | bytes 1572864 | tf_op jit(solution)/shard_map/psum | solution.py:238
  140.2 110.1 %copy-start.43 = (f32[128]{0:T(128)}, f32[128]{0:T(128)S(1)}, u32[]{:S(2)}) copy-start(f32[128]{0:T(128)S(1)} %tile.32) | copy-start | bytes 1540
  172.3 80.0 %copy-start.37 = (f32[3]{0:T(128)}, f32[3]{0:T(128)S(1)}, u32[]{:S(2)}) copy-start(f32[3]{0:T(128)S(1)} %fusion.51) | copy-start | bytes 40
  173.4 226.7 %all-reduce.16.cloned.1.call-start = ((), (), s32[]{:S(2)}) async-start(), calls=%async_computation.3 | async-start | bytes 655360 | tf_op jit(solution)/shard_map/psum | solution.py:258
  214.0 44.8 %copy-start.40 = (f32[16,2,2]{0,2,1:T(2,128)S(1)}, f32[16,2,2]{0,2,1:T(2,128)}, u32[]{:S(2)}) copy-start(f32[16,2,2]{0,2,1:T(2,128)} %copy-done.39) | copy-start | bytes 772
  214.0 44.8 %copy-start.42 = (f32[16,2,2]{0,2,1:T(2,128)S(1)}, f32[16,2,2]{0,2,1:T(2,128)}, u32[]{:S(2)}) copy-start(f32[16,2,2]{0,2,1:T(2,128)} %copy-done.41) | copy-start | bytes 772
  252.3 0.7 copy-start.6
  289.0 6.4 %copy-start.13 = (bf16[1,8,128,32]{2,3,1,0:T(8,128)(2,1)S(1)}, bf16[1,8,128,32]{2,3,1,0:T(8,128)(2,1)}, u32[]{:S(2)}) copy-start(bf16[1,8,128,32]{2,3,1,0:T(8,128)(2,1)} %get-tuple-element.133) | copy-start | bytes 196612
  289.0 6.5 %copy-start.14 = (bf16[1,8,128,32]{2,3,1,0:T(8,128)(2,1)S(1)}, bf16[1,8,128,32]{2,3,1,0:T(8,128)(2,1)}, u32[]{:S(2)}) copy-start(bf16[1,8,128,32]{2,3,1,0:T(8,128)(2,1)} %add_convert_fusion.1) | copy-start | bytes 196612
  295.8 0.8 copy-start.4
  307.8 2.8 copy-start.28
  307.9 2.8 copy-start.29
  323.5 1.5 copy-start.36
  324.1 4.0 copy-start.10
  324.1 4.0 copy-start.38
  325.9 1.5 copy-start.9
  326.0 111.9 %copy-start.7 = (f32[512,1,128]{2,0,1:T(8,128)S(1)}, f32[512,1,128]{2,0,1:T(8,128)}, u32[]{:S(2)}) copy-start(f32[512,1,128]{2,0,1:T(8,128)} %copy-done.6) | copy-start | bytes 786436
  326.0 111.9 %copy-start.44 = (f32[128]{0:T(128)S(1)}, f32[128]{0:T(128)}, u32[]{:S(2)}) copy-start(f32[128]{0:T(128)} %copy-done.43) | copy-start | bytes 1540
  326.0 111.9 %copy-start.45 = (f32[128]{0:T(128)S(1)}, f32[128]{0:T(128)}, u32[]{:S(2)}) copy-start(f32[128]{0:T(128)} %broadcast_multiply_fusion.4) | copy-start | bytes 1540
  328.1 108.5 %all-reduce.12.cloned.1.call-start = ((), (), s32[]{:S(2)}) async-start(), calls=%async_computation.1 | async-start | bytes 1572864 | tf_op jit(solution)/shard_map/psum | solution.py:238
  329.2 146.0 %all-reduce.14.cloned.1.call-start = ((), (), s32[]{:S(2)}) async-start(), calls=%async_computation.2 | async-start | bytes 1572864 | tf_op jit(solution)/shard_map/psum | solution.py:238
  (3 other events, 1.8 us)
Sparse Core Ops, SparseCore 0:
  139.5 72.8 all-reduce.17
  214.8 34.1 all-reduce.9
  328.2 71.7 all-reduce.15
  402.3 34.2 all-reduce.11
  440.1 35.0 all-reduce.13
where the time goes:
time: 491 us; the launch traced here: 485 us
  waiting for transfers between devices  213 us (43%)
  local copies, waits for them, and re-layouts  108 us (22%)
  other arithmetic  72.5 us (15%)
  blocking collectives  63.7 us (13%)
  between operations  18.7 us (4%)
  matrix products  9 us (2%)
    psum x2, waiting for transfers between devices, per_device(): gradient, curvature = lax.psum((grad_full, curv_full), 'pair')  109 us
    psum x3, waiting for transfers between devices, every_consensus(): lax.psum(project(current + dual_now / penalty_full, poly_basis), 'chan')  104 us
    all_gather x1, blocking collectives, per_device(): lax.all_gather(jones_init, 'pair', axis=0, tiled=True)  32.8 us
    all_gather x1, blocking collectives, per_device(): lax.all_gather(dual_init, 'pair', axis=0, tiled=True)  31 us
    mul x20, local copies, waits for them, and re-layouts, rotate_flat(): out_re = cosines * part_re - sines * part_im  30.3 us
    reduce_sum x4, other arithmetic, unrotate(): grad_re = -jnp.sum(neg_re * cosines + neg_im * sines, axis=1)  26.9 us
  transfers between devices with their start and end apart: 5, of which 5 were waited for; matrix products, arithmetic and copies ran while one was open for 2% of the time, Pallas kernels for 0%

commit v1 on v0

--- a/solution.py
+++ b/solution.py
@@ -12,6 +12,7 @@
 ITERS = 2
 STEP_SCALE = 0.3
 FULL_PRECISION = lax.Precision.HIGHEST
+build_terms = lambda here_x: jnp.sum(lax.all_gather(here_x, axis_name="chan"), 0)
 
 
 def pair_tables(block_count):
@@ -235,7 +236,7 @@
     tables = (jnp.asarray(row_table), jnp.asarray(col_table))
 
     def every_consensus(current, dual_now):
-        return lax.psum(project(current + dual_now / penalty_full, poly_basis), "chan")
+        return build_terms(project(current + dual_now / penalty_full, poly_basis))
 
     jones_now, duals_now = (
         lax.all_gather(jones_init, "pair", axis=0, tiled=True),

time: 491 us -> 419 us (0.85)
  waiting for transfers between devices: 213 us -> 136 us
    psum x3 -> x0, waiting for transfers between devices: 104 us -> none  [every_consensus(): lax.psum(project(current + dual_now / penalty_full, poly_basis), 'chan')]
    all_gather x0 -> x3, waiting for transfers between devices: none -> 27.7 us  [lax.all_gather(here_x, axis_name='chan')]
    reduce_sum x0 -> x3, other arithmetic: none -> 7.35 us  [jnp.sum(lax.all_gather(here_x, axis_name='chan'), 0)]
  transfers between devices with their start and end apart: 5 -> 5, of which waited for: 5 -> 3; matrix products, arithmetic and copies ran while one was open for 2% -> 2% of each run, Pallas kernels for 0% -> 0%
where the time goes in v1:
time: 419 us; the launch traced here: 414 us
  waiting for transfers between devices  136 us (32%)
  local copies, waits for them, and re-layouts  107 us (26%)
  other arithmetic  76.4 us (18%)
  blocking collectives  63.7 us (15%)
  between operations  20.6 us (5%)
  matrix products  9.01 us (2%)
    psum x2, waiting for transfers between devices, per_device(): gradient, curvature = lax.psum((grad_full, curv_full), 'pair')  108 us
    all_gather x1, blocking collectives, per_device(): lax.all_gather(jones_init, 'pair', axis=0, tiled=True)  32.8 us
    all_gather x1, blocking collectives, per_device(): lax.all_gather(dual_init, 'pair', axis=0, tiled=True)  31 us
    mul x20, local copies, waits for them, and re-layouts, rotate_flat(): out_re = cosines * part_re - sines * part_im  30.3 us
    all_gather x3, waiting for transfers between devices, lax.all_gather(here_x, axis_name='chan')  27.7 us
    reduce_sum x4, other arithmetic, unrotate(): grad_re = -jnp.sum(neg_re * cosines + neg_im * sines, axis=1)  26.9 us
    dot_general x2, local copies, waits for them, and re-layouts, slot_terms(): jnp.einsum('ftcpq,ftcpk->ftqk', residual, col_rhs, preferred_element_type...  9.01 us
    dot_general x2, local copies, waits for them, and re-layouts, slot_terms(): jnp.einsum('ftcpq,ftcqk->ftpk', residual, row_rhs, preferred_element_type...  8.76 us
  transfers between devices with their start and end apart: 5, of which 3 were waited for; matrix products, arithmetic and copies ran while one was open for 2% of the time, Pallas kernels for 0%

profile of v1, /device:TPU:0, one launch (start us, length us, event | category | flops | bytes accessed | tf_op | source)
XLA Modules:
  0.0 413.5 jit_solution(17554304990071902723)
XLA Ops:
  12.7 32.8 %all_gather.18 = f32[512,1,128]{2,1,0:T(1,128)S(1)} all-gather(f32[64,1,128]{2,1,0:T(1,128)} %param.11), channel_id=1, replica_groups=mesh['pair'=8,'chan'=4] {'pair'}, dimensions={0}, use_global_device_ids=true | all-gather | bytes 294912 | tf_op jit(solution)/shard_map/all_gather | solution.py:242
  48.8 2.9 cosine_reduce_fusion
  62.5 2.4 mul.1678
  64.9 2.7 copy.299
  68.0 2.4 mul.1684
  70.4 2.7 copy.302
  76.4 2.5 broadcast_in_dim.77
  79.0 4.2 %mul.1672 = f32[128,128]{1,0:T(8,128)S(1)} reshape(f32[64,2,64,2]{3,2,1,0:T(8,128)} %broadcast_in_dim.77) | data formatting | bytes 131072 | tf_op jit(solution)/shard_map/while/body/eval_jaxpr/mul | solution.py:113
  89.6 4.4 %copy.330 = f32[8,128,64]{0,2,1:T(8,128)} copy(f32[8,128,64]{1,2,0:T(8,128)S(1)} %convolution_bitcast_fusion.5) | data formatting | bytes 524288 | tf_op jit(solution)/shard_map/while/body/eval_jaxpr/ftcpq,ftcpk->ftqk/dot_general | solution.py:122
  94.0 7.2 %add_reduce_fusion.2 = (f32[64,2,16,2]{3,2,1,0:T(8,128)S(1)}, f32[64,2,16,2]{3,2,1,0:T(8,128)}) fusion(f32[1,8,64,2,2,16,2]{1,6,5,4,3,2,0:T(2,128)} %bitcast.414, f32[8,64,16]{0,2,1:T(8,128)S(1)} %bitcast.426, f32[8,64,16]{0,2,1:T(8,128)S(1)} %bitcast.423), kind=kLoop, calls=%fused_computation.13 | loop fusion | flops 253952 | bytes 360448 | tf_op jit(solution)/shard_map/while/body/eval_jaxpr/reduce_sum | solution.py:88
  102.3 2.4 copy.332
  104.7 2.3 negate_bitcast_fusion.4
  107.0 2.4 copy.333
  112.2 4.4 %copy.323 = f32[8,128,64]{0,2,1:T(8,128)} copy(f32[8,128,64]{1,2,0:T(8,128)S(1)} %convolution_bitcast_fusion.3) | data formatting | bytes 524288 | tf_op jit(solution)/shard_map/while/body/eval_jaxpr/ftcpq,ftcqk->ftpk/dot_general | solution.py:121
  116.6 7.4 %add_reduce_fusion.3 = (f32[64,2,16,2]{3,2,1,0:T(8,128)S(1)}, f32[64,2,16,2]{3,2,1,0:T(8,128)}) fusion(f32[1,8,64,2,2,16,2]{1,6,5,4,3,2,0:T(2,128)} %bitcast.415, f32[8,64,16]{0,2,1:T(8,128)S(1)} %bitcast.420, f32[8,64,16]{0,2,1:T(8,128)S(1)} %bitcast.417), kind=kLoop, calls=%fused_computation.15 | loop fusion | flops 253952 | bytes 360448 | tf_op jit(solution)/shard_map/while/body/eval_jaxpr/reduce_sum | solution.py:88
  125.0 1.8 copy.325
  126.8 2.3 negate_bitcast_fusion.6
  129.1 1.8 copy.326
  136.7 2.1 fusion.13
  141.1 31.0 %all_gather.19 = f32[512,1,128]{2,1,0:T(1,128)S(1)} all-gather(f32[64,1,128]{2,1,0:T(1,128)} %param.12), channel_id=1, replica_groups=mesh['pair'=8,'chan'=4] {'pair'}, dimensions={0}, use_global_device_ids=true | all-gather | bytes 294912 | tf_op jit(solution)/shard_map/all_gather | solution.py:243
  174.8 38.5 %all-reduce.9.cloned.1.call-done = (f32[512,1,128]{2,0,1:T(8,128)}, f32[512,32]{0,1:T(8,128)}) async-done(((f32[512,1,128]{2,0,1:T(8,128)}, f32[512,32]{0,1:T(8,128)}), (f32[512,1,128]{2,0,1:T(8,128)}, f32[512,32]{0,1:T(8,128)})) %all-reduce.9.cloned.1.call-update) | async-done | bytes 327696 | tf_op jit(solution)/shard_map/psum | solution.py:259
  214.9 1.8 copy.343
  216.7 3.0 reduce_sum.339
  221.0 1.9 add_bitcast_fusion.1
  231.0 2.1 copy.354
  233.1 1.7 mul.1785
  234.8 2.1 copy.356
  237.0 2.3 mul.1790
  239.3 1.7 fusion.58
  240.9 1.6 add_convert_fusion.1
  242.5 2.1 copy.360
  244.7 1.7 mul.1802
  246.4 2.1 copy.362
  248.5 2.3 mul.1807
  250.8 2.1 copy.346
  252.9 2.3 mul.1771
  255.2 2.1 copy.348
  257.4 2.3 mul.1774
  259.7 1.6 subtract_convert_fusion
  261.3 1.6 fusion.59
  267.6 4.6 %copy.376 = f32[8,128,64]{0,2,1:T(8,128)} copy(f32[8,128,64]{1,2,0:T(8,128)S(1)} %convolution_bitcast_fusion.4) | data formatting | bytes 524288 | tf_op jit(solution)/shard_map/while/body/eval_jaxpr/ftcpq,ftcpk->ftqk/dot_general | solution.py:122
  272.2 6.2 %add_reduce_fusion = (f32[64,2,16,2]{3,2,1,0:T(8,128)S(1)}, f32[64,2,16,2]{3,2,1,0:T(8,128)S(1)}) fusion(f32[1,8,64,2,2,16,2]{1,6,5,4,3,2,0:T(2,128)} %bitcast.412, f32[8,64,16]{0,2,1:T(8,128)S(1)} %bitcast.427, f32[8,64,16]{0,2,1:T(8,128)S(1)} %bitcast.424), kind=kLoop, calls=%fused_computation.9 | loop fusion | flops 253952 | bytes 360448 | tf_op jit(solution)/shard_map/while/body/eval_jaxpr/reduce_sum | solution.py:88
  283.5 4.4 %copy.368 = f32[8,128,64]{0,2,1:T(8,128)} copy(f32[8,128,64]{1,2,0:T(8,128)S(1)} %convolution_bitcast_fusion.2) | data formatting | bytes 524288 | tf_op jit(solution)/shard_map/while/body/eval_jaxpr/ftcpq,ftcqk->ftpk/dot_general | solution.py:121
  287.9 6.2 %add_reduce_fusion.1 = (f32[64,2,16,2]{3,2,1,0:T(8,128)S(1)}, f32[64,2,16,2]{3,2,1,0:T(8,128)S(1)}) fusion(f32[1,8,64,2,2,16,2]{1,6,5,4,3,2,0:T(2,128)} %bitcast.413, f32[8,64,16]{0,2,1:T(8,128)S(1)} %bitcast.421, f32[8,64,16]{0,2,1:T(8,128)S(1)} %bitcast.418), kind=kLoop, calls=%fused_computation.11 | loop fusion | flops 253952 | bytes 360448 | tf_op jit(solution)/shard_map/while/body/eval_jaxpr/reduce_sum | solution.py:88
  299.8 70.0 %all-reduce.7.cloned.1.call-done = (f32[512,32]{0,1:T(8,128)}, f32[512,1,128]{2,0,1:T(8,128)}) async-done(((f32[512,32]{0,1:T(8,128)}, f32[512,1,128]{2,0,1:T(8,128)}), (f32[512,32]{0,1:T(8,128)}, f32[512,1,128]{2,0,1:T(8,128)})) %all-reduce.7.cloned.1.call-update) | async-done | bytes 327696 | tf_op jit(solution)/shard_map/psum | solution.py:259
  370.9 2.2 reduce_sum.355
  374.4 27.7 %all-gather.8.cloned.1.call-done = f32[4,512,3,128]{3,1,2,0:T(8,128)} async-done(((f32[1,512,3,128]{3,1,2,0:T(8,128)}), f32[4,512,3,128]{3,1,2,0:T(8,128)}) %all-gather.8.cloned.1.call-update) | async-done | bytes 3145744 | tf_op jit(solution)/shard_map/all_gather | solution.py:15
  402.1 2.1 reduce_sum.362
  (235 shorter events, 70.4 us)
Async XLA Ops:
  8.0 205.3 %all-reduce.9.cloned.1.call-start = ((), (), s32[]{:S(2)}) async-start(), calls=%async_computation.4 | async-start | bytes 655360 | tf_op jit(solution)/shard_map/psum | solution.py:259
  45.5 1.0 copy-start.3
  47.0 1.8 copy-start.17
  47.0 1.8 copy-start.19
  47.0 11.5 %copy-start.21 = (f32[64,2,16,2]{0,2,3,1:T(8,128)}, f32[64,2,16,2]{0,2,3,1:T(8,128)S(1)}, u32[]{:S(2)}) copy-start(f32[64,2,16,2]{0,2,3,1:T(8,128)S(1)} %get-tuple-element.97) | copy-start | bytes 49156
  47.0 12.4 %copy-start.23 = (f32[64,2,16,2]{0,2,3,1:T(8,128)}, f32[64,2,16,2]{0,2,3,1:T(8,128)S(1)}, u32[]{:S(2)}) copy-start(f32[64,2,16,2]{0,2,3,1:T(8,128)S(1)} %get-tuple-element.112) | copy-start | bytes 49156
  47.0 1.8 copy-start.35
  54.4 3.5 copy-start.1
  57.2 3.1 copy-start.2
  58.5 1.8 copy-start.32
  60.3 1.8 copy-start.34
  62.4 5.1 %copy-start.33 = (f32[8,1024]{1,0:T(8,128)S(1)}, f32[8,1024]{1,0:T(8,128)}, u32[]{:S(2)}) copy-start(f32[8,1024]{1,0:T(8,128)} %get-tuple-element.117) | copy-start | bytes 98308
  70.4 5.3 %copy-start.22 = (f32[64,2,16,2]{0,2,3,1:T(8,128)S(1)}, f32[64,2,16,2]{0,2,3,1:T(8,128)}, u32[]{:S(2)}) copy-start(f32[64,2,16,2]{0,2,3,1:T(8,128)} %copy-done.21) | copy-start | bytes 49156
  70.4 5.4 %copy-start.24 = (f32[64,2,16,2]{0,2,3,1:T(8,128)S(1)}, f32[64,2,16,2]{0,2,3,1:T(8,128)}, u32[]{:S(2)}) copy-start(f32[64,2,16,2]{0,2,3,1:T(8,128)} %copy-done.23) | copy-start | bytes 49156
  70.4 6.0 %copy-start.18 = (f32[64,2,16,2]{0,2,3,1:T(8,128)S(1)}, f32[64,2,16,2]{0,2,3,1:T(8,128)}, u32[]{:S(2)}) copy-start(f32[64,2,16,2]{0,2,3,1:T(8,128)} %copy-done.17) | copy-start | bytes 49156
  70.4 6.0 %copy-start.20 = (f32[64,2,16,2]{0,2,3,1:T(8,128)S(1)}, f32[64,2,16,2]{0,2,3,1:T(8,128)}, u32[]{:S(2)}) copy-start(f32[64,2,16,2]{0,2,3,1:T(8,128)} %copy-done.19) | copy-start | bytes 49156
  73.1 5.8 %copy-start = (f32[1,8,128,32]{2,3,1,0:T(8,128)}, f32[1,8,128,32]{2,3,1,0:T(8,128)S(1)}, u32[]{:S(2)}) copy-start(f32[1,8,128,32]{2,3,1,0:T(8,128)S(1)} %copy.302) | copy-start | bytes 393220
  78.9 5.6 %copy-start.15 = (bf16[1,1,8,2,128,128]{5,4,3,2,1,0:T(8,128)(2,1)S(1)}, bf16[1,1,8,2,128,128]{5,4,3,2,1,0:T(8,128)(2,1)}, u32[]{:S(2)}) copy-start(bf16[1,1,8,2,128,128]{5,4,3,2,1,0:T(8,128)(2,1)} %param.15) | copy-start | bytes 1572868
  78.9 8.2 %copy-start.11 = (bf16[1,8,128,32]{2,3,1,0:T(8,128)(2,1)S(1)}, bf16[1,8,128,32]{2,3,1,0:T(8,128)(2,1)}, u32[]{:S(2)}) copy-start(bf16[1,8,128,32]{2,3,1,0:T(8,128)(2,1)} %get-tuple-element.141) | copy-start | bytes 196612
  78.9 8.2 %copy-start.12 = (bf16[1,8,128,32]{2,3,1,0:T(8,128)(2,1)S(1)}, bf16[1,8,128,32]{2,3,1,0:T(8,128)(2,1)}, u32[]{:S(2)}) copy-start(bf16[1,8,128,32]{2,3,1,0:T(8,128)(2,1)} %add_convert_fusion.4) | copy-start | bytes 196612
  78.9 8.2 %copy-start.30 = (bf16[1,8,128,32]{2,3,1,0:T(8,128)(2,1)S(1)}, bf16[1,8,128,32]{2,3,1,0:T(8,128)(2,1)}, u32[]{:S(2)}) copy-start(bf16[1,8,128,32]{2,3,1,0:T(8,128)(2,1)} %get-tuple-element.140) | copy-start | bytes 196612
  88.5 0.8 copy-start.5
  102.3 8.6 %copy-start.25 = (bf16[1,8,128,32]{2,3,1,0:T(8,128)(2,1)S(1)}, bf16[1,8,128,32]{2,3,1,0:T(8,128)(2,1)}, u32[]{:S(2)}) copy-start(bf16[1,8,128,32]{2,3,1,0:T(8,128)(2,1)} %get-tuple-element.142) | copy-start | bytes 196612
  102.3 8.6 %copy-start.26 = (bf16[1,8,128,32]{2,3,1,0:T(8,128)(2,1)S(1)}, bf16[1,8,128,32]{2,3,1,0:T(8,128)(2,1)}, u32[]{:S(2)}) copy-start(bf16[1,8,128,32]{2,3,1,0:T(8,128)(2,1)} %get-tuple-element.143) | copy-start | bytes 196612
  102.3 8.6 %copy-start.27 = (bf16[1,8,128,32]{2,3,1,0:T(8,128)(2,1)S(1)}, bf16[1,8,128,32]{2,3,1,0:T(8,128)(2,1)}, u32[]{:S(2)}) copy-start(bf16[1,8,128,32]{2,3,1,0:T(8,128)(2,1)} %get-tuple-element.156) | copy-start | bytes 196612
  125.0 6.6 %copy-start.36 = (f32[64,16,2]{0,1,2:T(8,128)S(1)}, f32[64,16,2]{0,1,2:T(8,128)}, u32[]{:S(2)}) copy-start(f32[64,16,2]{0,1,2:T(8,128)} %add_reduce_fusion.11) | copy-start | bytes 24580
  133.2 7.0 %copy-start.8 = (f32[512,1,128]{2,0,1:T(8,128)}, f32[512,1,128]{2,0,1:T(8,128)S(1)}, u32[]{:S(2)}) copy-start(f32[512,1,128]{2,0,1:T(8,128)S(1)} %add_dynamic-update-slice_fusion.1) | copy-start | bytes 786436
  140.3 76.4 %all-gather.4.cloned.1.call-start = ((), (), s32[]{:S(2)}) async-start(), calls=%async_computation | async-start | bytes 3932160 | tf_op jit(solution)/shard_map/all_gather | solution.py:15
  141.1 79.9 %copy-start.44 = (f32[128]{0:T(128)}, f32[128]{0:T(128)S(1)}, u32[]{:S(2)}) copy-start(f32[128]{0:T(128)S(1)} %tile.32) | copy-start | bytes 1540
  173.1 46.5 %copy-start.38 = (f32[3]{0:T(128)}, f32[3]{0:T(128)S(1)}, u32[]{:S(2)}) copy-start(f32[3]{0:T(128)S(1)} %fusion.51) | copy-start | bytes 40
  174.2 195.6 %all-reduce.7.cloned.1.call-start = ((), (), s32[]{:S(2)}) async-start(), calls=%async_computation.3 | async-start | bytes 655360 | tf_op jit(solution)/shard_map/psum | solution.py:259
  219.7 9.7 %copy-start.41 = (f32[16,2,2]{0,2,1:T(2,128)S(1)}, f32[16,2,2]{0,2,1:T(2,128)}, u32[]{:S(2)}) copy-start(f32[16,2,2]{0,2,1:T(2,128)} %copy-done.40) | copy-start | bytes 772
  219.7 9.7 %copy-start.43 = (f32[16,2,2]{0,2,1:T(2,128)S(1)}, f32[16,2,2]{0,2,1:T(2,128)}, u32[]{:S(2)}) copy-start(f32[16,2,2]{0,2,1:T(2,128)} %copy-done.42) | copy-start | bytes 772
  259.7 6.4 %copy-start.13 = (bf16[1,8,128,32]{2,3,1,0:T(8,128)(2,1)S(1)}, bf16[1,8,128,32]{2,3,1,0:T(8,128)(2,1)}, u32[]{:S(2)}) copy-start(bf16[1,8,128,32]{2,3,1,0:T(8,128)(2,1)} %get-tuple-element.133) | copy-start | bytes 196612
  259.7 6.5 %copy-start.14 = (bf16[1,8,128,32]{2,3,1,0:T(8,128)(2,1)S(1)}, bf16[1,8,128,32]{2,3,1,0:T(8,128)(2,1)}, u32[]{:S(2)}) copy-start(bf16[1,8,128,32]{2,3,1,0:T(8,128)(2,1)} %add_convert_fusion.1) | copy-start | bytes 196612
  266.5 0.8 copy-start.4
  278.5 2.8 copy-start.28
  278.5 2.8 copy-start.29
  294.1 1.5 copy-start.37
  294.8 4.0 copy-start.10
  294.8 4.0 copy-start.39
  296.6 1.5 copy-start.9
  298.7 72.2 %all-gather.6.cloned.1.call-start = ((), (), s32[]{:S(2)}) async-start(), calls=%async_computation.1 | async-start | bytes 3932160 | tf_op jit(solution)/shard_map/all_gather | solution.py:15
  299.8 102.3 %all-gather.8.cloned.1.call-start = ((), (), s32[]{:S(2)}) async-start(), calls=%async_computation.2 | async-start | bytes 3932160 | tf_op jit(solution)/shard_map/all_gather | solution.py:15
  370.8 2.4 copy-start.7
  370.8 2.4 copy-start.31
  370.8 2.4 copy-start.45
  370.8 2.4 copy-start.46
  (4 other events, 2.5 us)
Sparse Core Ops, SparseCore 0:
  140.4 72.8 all-reduce.8
  298.8 70.9 all-reduce.6
Sparse Core Ops, SparseCore 1:
  174.3 29.9 all-gather.3
  300.7 27.6 all-gather.5
  374.5 27.6 all-gather.7
